TPU v7x, 512 devices: a whole 4x4x16 slice. The times are simulated.
512 devices in a mesh: dp: 32 (over y, x, core), fsdp: 16 (over z).
Axes of the slice: x: 4, y: 4, z: 16, core: 2. Of those that a mesh axis runs over, the one named last changes fastest.
Arguments:
- queries: bfloat16 [131072, 2048], P(('dp', 'fsdp')), may hold values from -600 to 600
- w_kv: bfloat16 [2, 2048, 896], P(None, 'fsdp'), may hold values from -0.1875 to 0.1875
- encodings: bfloat16 [196608, 896], P(('dp', 'fsdp')), may hold values from -6 to 6
- counts: int32 [512], P(('dp', 'fsdp')), may hold values from 48 to 384, as said below
- owner_rank: int32 [196608], P(('dp', 'fsdp')), may hold values from 0 to 31, as said below
- owner_span: int32 [196608], P(('dp', 'fsdp')), may hold values from 0 to 3, as said below
- grad_ctx: bfloat16 [131072, 2048], P(('dp', 'fsdp')), may hold values from -24 to 24
Outputs:
- grad_queries: bfloat16 [131072, 2048], P(('dp', 'fsdp'))
- grad_value: bfloat16 [2048, 896], P('fsdp')
Inputs may be any that keep to these rules, and one draw needn't show every extreme that they name: `counts`: each count is 384 divided by 1, 2, 4 or 8; among the devices of equal fsdp index one holds 384. `owner_rank`: among the live rows of one device at most 12 name the same owner; a device whose count is 384 names every owner exactly 12 times. `owner_span`: every span of every decoder device is named by at least one live row of a device with equal fsdp index.
All inputs are finite; a program needn't handle non-finite values.
Results may differ from a plain program's by a relative error of at most 0.023.
Values may be sent and summed in bfloat16 or wider, within the bound.
No kernel may reach another device: no remote copies, remote signals or barrier semaphores. Data moves between devices by JAX's collectives and lax.ppermute only.
A program may use at most 64 MiB of HBM per device.

v0:
```python
import jax
import jax.numpy as jnp
from jax import lax
from jax.experimental import pallas as pl
from jax.experimental.pallas import tpu as pltpu
from jax.sharding import Mesh
from jax.sharding import PartitionSpec as P

HEADS = 16
HEAD_DIM = 128
SPAN = 64
ENC = 896
TOK = 256
ROWS = 384
DP = 32
CAP = 12
PLANE = 16
EXT = ENC + 128
BIG = 2.0**100
SCALE = 1.0 / HEAD_DIM**0.5
LOG2E = 1.4426950408889634


NN = (((1,), (0,)), ((), ()))
NT = (((1,), (1,)), ((), ()))
TN = (((0,), (0,)), ((), ()))


def dot(a, b, dims):
    return lax.dot_general(a, b, dims, preferred_element_type=jnp.float32)


def pack_body(count_ref, rank_ref, span_ref, enc_ref, out_ref):
    rank = rank_ref[...].reshape(1, ROWS)
    live = lax.broadcasted_iota(jnp.int32, (1, ROWS), 1) < count_ref[0]
    owner = lax.broadcasted_iota(jnp.int32, (DP, ROWS), 0)
    hit = ((owner == rank) & live).astype(jnp.float32)
    earlier = lax.broadcasted_iota(jnp.int32, (ROWS, ROWS), 0) < lax.broadcasted_iota(jnp.int32, (ROWS, ROWS), 1)
    before = dot(hit.astype(jnp.bfloat16), earlier.astype(jnp.float32).astype(jnp.bfloat16), NN)
    slot = jnp.sum(before * hit, axis=0, keepdims=True).astype(jnp.int32)
    target = jnp.where(live, rank * CAP + slot, -1)
    place = (lax.broadcasted_iota(jnp.int32, (ROWS, ROWS), 0) == target).astype(jnp.float32).astype(jnp.bfloat16)
    spans = (lax.broadcasted_iota(jnp.int32, (128, ROWS), 0) == span_ref[...].reshape(1, ROWS)).astype(jnp.float32).astype(jnp.bfloat16)
    out_ref[:, :ENC] = dot(place, enc_ref[...], NN).astype(jnp.bfloat16)
    out_ref[:, ENC:] = dot(place, spans, NT).astype(jnp.bfloat16)


def pack(counts, rank, span, enc, interpret=False):
    vmem = pl.BlockSpec(memory_space=pltpu.VMEM)
    return pl.pallas_call(
        pack_body,
        out_shape=jax.ShapeDtypeStruct((ROWS, EXT), jnp.bfloat16),
        in_specs=[pl.BlockSpec(memory_space=pltpu.SMEM), vmem, vmem, vmem],
        out_specs=vmem,
        interpret=interpret,
        name="pack",
    )(counts, rank, span, enc)


NEAR = ((2, -2, 0), (1, -1, 3), (1, -1, -3))
FAR = ((4, -4, 6, -6, 8), (-3, 5, -5, 7, -7), (3, 5, -5, 7, -7))


def choose(i, options):
    if isinstance(i, int):
        return options[i]
    result = options[-1]
    for k in range(len(options) - 2, -1, -1):
        result = jnp.where(i == k, options[k], result)
    return result


def head_of(i, place, offsets, other=False):
    c, z = place[0] >> 4, place[0] & (HEADS - 1)
    if other:
        c = 1 - c
    even, first, second = (choose(i, row) for row in offsets)
    turn = jnp.where((c + z) & 1 == 0, even, jnp.where(c == 0, first, second))
    return (z + turn) & (HEADS - 1)


def attend_step(rows_ref, mask_ref, q_ref, g_ref, q2_ref, g2_ref, w_ref, gq_ref, gq2_ref, part_ref, dval_ref):
    step = pl.program_id(0)
    group = part_ref.shape[1]
    rows = rows_ref[...]
    pair = dot(rows, w_ref[...], NT).astype(jnp.bfloat16)
    token = lax.broadcasted_iota(jnp.int32, (TOK, 128), 0)
    spans = (lax.broadcasted_iota(jnp.int32, (TOK, 128), 1) == token // SPAN).astype(jnp.float32).astype(jnp.bfloat16)
    spots = []
    for k, (q_ref_, g_ref_, out_ref) in enumerate(((q_ref, g_ref, gq_ref), (q2_ref, g2_ref, gq2_ref))):
        at = slice(k * ROWS, (k + 1) * ROWS)
        key, value, g = pair[at, :HEAD_DIM], pair[at, HEAD_DIM:], g_ref_[...]
        scores = dot(jnp.concatenate([q_ref_[...], spans], 1), jnp.concatenate([key, mask_ref[at, :]], 1), NT)
        spots.append((at, key, g, scores, dot(g, value, NT), out_ref))
    for at, key, g, scores, dprob, out_ref in spots:
        highest = jnp.max(scores, axis=1, keepdims=True)
        weights = jnp.exp2((scores - highest) * (SCALE * LOG2E))
        probs = weights * (1.0 / jnp.sum(weights, axis=1, keepdims=True))
        low = probs.astype(jnp.bfloat16)
        delta = jnp.sum(low.astype(jnp.float32) * dprob, axis=1, keepdims=True)
        dscore = (probs * (dprob - delta)).astype(jnp.bfloat16)
        out_ref[...] = (dot(dscore, key, NN) * SCALE).astype(jnp.bfloat16)
        turned = dot(g, low, TN).astype(jnp.bfloat16)
        dval_ref[pl.ds(pl.multiple_of(step * HEAD_DIM, HEAD_DIM), HEAD_DIM), at] = turned

    @pl.when(step == group - 1)
    def _():
        partial = dot(dval_ref[...], rows, NN)
        for j in range(group):
            block = partial[j * HEAD_DIM : (j + 1) * HEAD_DIM]
            part_ref[:, j, :, :] = block.reshape(PLANE, 8, ENC).astype(jnp.bfloat16)


def near_body(
    place_ref, own_ref, other_ref, q_ref, g_ref, q2_ref, g2_ref, w0_ref, w1_ref, w2_ref,
    gq_ref, gq2_ref, part_ref, rows_ref, mask_ref, w_ref, dval_ref,
):
    step = pl.program_id(0)

    @pl.when(step == 0)
    def _():
        row = lax.broadcasted_iota(jnp.int32, (ROWS, ROWS), 0)
        col = lax.broadcasted_iota(jnp.int32, (ROWS, ROWS), 1)
        second = row // (ROWS // 2)
        rest = row - second * (ROWS // 2)
        chip = rest // CAP
        owner = jnp.where(place_ref[0] < HEADS, second, 1 - second)
        source = chip * (2 * CAP) + owner * CAP + (rest - chip * CAP)
        select = (source == col).astype(jnp.float32).astype(jnp.bfloat16)
        lane = lax.broadcasted_iota(jnp.int32, (ROWS // 2, 128), 1)
        for k, ref in enumerate((own_ref, other_ref)):
            moved = dot(select, ref[...], NN)
            for p in range(2):
                part = moved[p * (ROWS // 2) : (p + 1) * (ROWS // 2)]
                at = pl.ds(p * ROWS + k * (ROWS // 2), ROWS // 2)
                rows_ref[at, :] = part[:, :ENC].astype(jnp.bfloat16)
                mask_ref[at, :] = jnp.where(lane < 4, (part[:, ENC:] - 1.0) * BIG, 0.0).astype(jnp.bfloat16)

    for j, ref in enumerate((w0_ref, w1_ref, w2_ref)):

        @pl.when(step == j)
        def _(ref=ref):
            w_ref[...] = ref[...].reshape(2 * HEAD_DIM, ENC)

    attend_step(rows_ref, mask_ref, q_ref, g_ref, q2_ref, g2_ref, w_ref, gq_ref, gq2_ref, part_ref, dval_ref)


def far_body(
    place_ref, rows_ref, mask_ref, q_ref, g_ref, q2_ref, g2_ref, wk_ref, wv_ref, a0, a1,
    gq_ref, gq2_ref, part_ref, w_ref, dval_ref,
):
    w_ref[:HEAD_DIM, :] = wk_ref[...].reshape(HEAD_DIM, ENC)
    w_ref[HEAD_DIM:, :] = wv_ref[...].reshape(HEAD_DIM, ENC)
    attend_step(rows_ref, mask_ref, q_ref, g_ref, q2_ref, g2_ref, w_ref, gq_ref, gq2_ref, part_ref, dval_ref)


WIDE = jax.ShapeDtypeStruct((TOK, HEADS * HEAD_DIM), jnp.bfloat16)


def whole(*shape):
    return pl.BlockSpec(shape, lambda i, place: (0,) * len(shape))


def head_block(offsets):
    return pl.BlockSpec((TOK, HEAD_DIM), lambda i, place: (0, head_of(i, place, offsets)))


def part_of(group):
    return jax.ShapeDtypeStruct((PLANE, group, 8, ENC), jnp.bfloat16)


def work(group):
    return [pltpu.VMEM((2 * HEAD_DIM, ENC), jnp.bfloat16), pltpu.VMEM((group * HEAD_DIM, 2 * ROWS), jnp.bfloat16)]


def attend_near(place, own, other, tokens, weights, interpret=False):
    head = head_block(NEAR)
    group = len(weights)
    return pl.pallas_call(
        near_body,
        grid_spec=pltpu.PrefetchScalarGridSpec(
            num_scalar_prefetch=1,
            grid=(group,),
            in_specs=[whole(ROWS, EXT)] * 2 + [head] * 4 + [whole(2, HEAD_DIM, ENC)] * group,
            out_specs=[head, head, whole(PLANE, group, 8, ENC), whole(2 * ROWS, ENC), whole(2 * ROWS, 128)],
            scratch_shapes=work(group),
        ),
        out_shape=[
            WIDE,
            WIDE,
            part_of(group),
            jax.ShapeDtypeStruct((2 * ROWS, ENC), jnp.bfloat16),
            jax.ShapeDtypeStruct((2 * ROWS, 128), jnp.bfloat16),
        ],
        interpret=interpret,
        name="near",
    )(place, own, other, *tokens, *weights)


def attend_far(place, rows, mask, tokens, weights, gq, gq2, interpret=False):
    head = head_block(FAR)
    group = weights.shape[2]
    kv = lambda pick: pl.BlockSpec((PLANE, 1, 1, 8, ENC), lambda i, place: (0, pick(place[0] >> 4), i, 0, 0))
    kept = pl.BlockSpec(memory_space=pl.ANY)
    return pl.pallas_call(
        far_body,
        grid_spec=pltpu.PrefetchScalarGridSpec(
            num_scalar_prefetch=1,
            grid=(group,),
            in_specs=[whole(2 * ROWS, ENC), whole(2 * ROWS, 128)]
            + [head] * 4
            + [kv(lambda c: c), kv(lambda c: 1 - c)]
            + [kept] * 2,
            out_specs=[head, head, whole(PLANE, group, 8, ENC)],
            scratch_shapes=work(group),
        ),
        out_shape=[WIDE, WIDE, part_of(group)],
        input_output_aliases={9: 0, 10: 1},
        interpret=interpret,
        name="far",
    )(place, rows, mask, *tokens, weights, weights, gq, gq2)


def deal_body(place_ref, heads_ref, kept_ref, given_ref):
    for i in range(len(FAR[0])):
        kept_ref[i] = heads_ref[head_of(i, place_ref, FAR)]
        given_ref[i] = heads_ref[head_of(i, place_ref, FAR, True)]


SMEM = pl.BlockSpec(memory_space=pltpu.SMEM)
VMEM = pl.BlockSpec(memory_space=pltpu.VMEM)


def deal(place, heads, interpret=False):
    shape = jax.ShapeDtypeStruct((len(FAR[0]), 8, ENC), jnp.bfloat16)
    return pl.pallas_call(
        deal_body, out_shape=[shape, shape], in_specs=[SMEM, VMEM], out_specs=[VMEM] * 2, interpret=interpret, name="deal"
    )(place, heads)


def arrange_body(place_ref, near_ref, far_ref, out_ref):
    for ref, offsets in ((near_ref, NEAR), (far_ref, FAR)):
        for i in range(len(offsets[0])):
            out_ref[head_of(i, place_ref, offsets)] = ref[i]


def arrange(place, near, far, interpret=False):
    shape = jax.ShapeDtypeStruct((HEADS, 8, ENC), jnp.bfloat16)
    return pl.pallas_call(
        arrange_body, out_shape=shape, in_specs=[SMEM, VMEM, VMEM], out_specs=VMEM, interpret=interpret, name="arrange"
    )(place, near, far)


def swap(array):
    return lax.ppermute(array, "c", [(0, 1), (1, 0)])


def exchange(array, axis):
    return lax.all_to_all(array, axis, split_axis=0, concat_axis=0, tiled=True)


def spread(array, axis, count):
    return exchange(jnp.broadcast_to(array[None], (count,) + array.shape), axis)


def total(array):
    return array.astype(jnp.float32).sum(0)


def fetch(array, turns):
    pairs = []
    for c in range(2):
        for z in range(HEADS):
            turn = turns[(c + z) % 2 * (1 + c)]
            core = 1 - c if (turn % 2 == 0) == (turns[0] != 0) else c
            pairs.append((core * HEADS + (z + turn) % HEADS, c * HEADS + z))
    assert len({source for source, _ in pairs}) == len(pairs)
    return lax.ppermute(array, ("c", "z"), pairs)


def local(queries, w_kv, encodings, counts, owner_rank, owner_span, grad_ctx):
    c = lax.axis_index("c")
    z = lax.axis_index("z")
    place = lax.axis_index(("c", "z")).astype(jnp.int32).reshape(1)
    plane = lax.axis_index("y") * 4 + lax.axis_index("x")
    piece = lax.dynamic_slice(w_kv, (c, plane * 8, 0), (1, 8, ENC))[0]
    heads = spread(piece, "z", HEADS)
    kept, given = deal(place, heads)
    mine = jnp.stack([kept, swap(given)])
    near = []
    for turns in zip(*NEAR):
        near.append(fetch(w_kv, turns))

    packed = pack(counts, owner_rank, owner_span, encodings)
    arrived = exchange(packed.reshape(PLANE, 2 * CAP, EXT), ("y", "x")).reshape(ROWS, EXT)
    other = swap(arrived)
    weights = spread(mine, ("y", "x"), PLANE)
    tokens = (queries, grad_ctx, swap(queries), swap(grad_ctx))

    gq, gq2, part, rows, mask = attend_near(place, arrived, other, tokens, near)
    near_part = exchange(part, ("y", "x"))
    gq, gq2, part = attend_far(place, rows, mask, tokens, weights, gq, gq2)
    far_part = exchange(part, ("y", "x"))

    sums = arrange(place, *(total(part).astype(jnp.bfloat16) for part in (near_part, far_part)))
    final = (total(exchange(sums, "z")) / DP).astype(jnp.bfloat16)
    own_head = (lax.broadcasted_iota(jnp.int32, gq.shape, 1) // HEAD_DIM) % 2 == c
    grad_queries, final = lax.optimization_barrier((jnp.where(own_head, gq, swap(gq2)), final))
    blocks = spread(final, ("y", "x", "c"), DP).reshape(PLANE, 2, 8, ENC)
    return grad_queries, lax.dynamic_index_in_dim(blocks, z % 2, 1, False).reshape(HEAD_DIM, ENC)


def solution(mesh):
    fine = Mesh(mesh.devices.reshape(4, 4, 2, HEADS), ("y", "x", "c", "z"))
    every = ("y", "x", "c", "z")
    in_specs = (
        P(every, None),
        P(None, "z", None),
        P(every, None),
        P(every),
        P(every),
        P(every),
        P(every, None),
    )
    out_specs = (P(every, None), P("z", None))
    return jax.shard_map(local, mesh=fine, in_specs=in_specs, out_specs=out_specs, check_vma=False)
```

profile of v0, /device:TPU:1, one launch (start us, length us, event | category | flops | bytes accessed | tf_op | source)
XLA Modules:
  0.0 201.1 jit_solution(3117636878816428915)
XLA Ops:
  2.1 15.7 %all-to-all-start.1 = ((bf16[16,8,896]{2,1,0:T(8,128)(2,1)}), bf16[16,8,896]{2,1,0:T(8,128)(2,1)S(1)}, u32[]{:S(2)}, u32[]{:S(2)}) async-start(bf16[16,8,896]{2,1,0:T(8,128)(2,1)} %broadcast_in_dim.9), calls=%async_computation.1 | async-start | bytes 458752 | tf_op jit(solution)/shard_map/all_to_all | solution.py:259
  18.5 2.8 %pack.1 = bf16[384,1024]{1,0:T(8,128)(2,1)} custom-call(s32[1]{0:T(128)S(6)} %copy.13.count_ref, s32[384]{0:T(512)} %rank_ref.1, s32[384]{0:T(512)} %span_ref.1, bf16[384,896]{1,0:T(8,128)(2,1)} %enc_ref.1), custom_call_target="tpu_custom_call" | custom-call | tf_op jit(solution)/shard_map/pack/pallas_call | solution.py:50
  21.2 9.2 %all-to-all-done.1.heads_ref = bf16[16,8,896]{2,1,0:T(8,128)(2,1)S(1)} async-done(((bf16[16,8,896]{2,1,0:T(8,128)(2,1)}), bf16[16,8,896]{2,1,0:T(8,128)(2,1)S(1)}, u32[]{:S(2)}, u32[]{:S(2)}) %all-to-all-start.1) | async-done | bytes 229408 | tf_op jit(solution)/shard_map/all_to_all | solution.py:259
  30.5 6.8 %all-to-all-start = ((bf16[16,24,1024]{2,1,0:T(8,128)(2,1)}), bf16[16,24,1024]{2,1,0:T(8,128)(2,1)S(1)}, u32[]{:S(2)}, u32[]{:S(2)}) async-start(bf16[16,24,1024]{2,1,0:T(8,128)(2,1)} %bitcast.12), calls=%async_computation | async-start | bytes 1572864 | tf_op jit(solution)/shard_map/all_to_all | solution.py:259
  38.9 7.6 %collective-permute-start.6 = (bf16[5,8,896]{2,1,0:T(8,128)(2,1)}, bf16[5,8,896]{2,1,0:T(8,128)(2,1)S(1)}, u32[]{:S(2)}, u32[]{:S(2)}) collective-permute-start(bf16[5,8,896]{2,1,0:T(8,128)(2,1)} %get-tuple-element.17), channel_id=1, source_target_pairs={{0,16},{16,0},{1,17},{17,1},{2,18},{18,2},{3,19},{19,3},{4,20},{20... | collective-permute-start | bytes 215048 | tf_op jit(solution)/shard_map/ppermute | solution.py:255
  50.2 7.1 %all-to-all-start.2 = ((bf16[16,2,5,8,896]{4,3,2,1,0:T(8,128)(2,1)}), bf16[16,2,5,8,896]{4,3,2,1,0:T(8,128)(2,1)S(1)}, u32[]{:S(2)}, u32[]{:S(2)}) async-start(bf16[16,2,5,8,896]{4,3,2,1,0:T(8,128)(2,1)} %broadcast_in_dim.10), calls=%async_computation.2 | async-start | bytes 4587520 | tf_op jit(solution)/shard_map/all_to_all | solution.py:259
  57.3 4.7 %collective-permute-start.1 = (bf16[256,2048]{1,0:T(8,128)(2,1)S(1)}, bf16[256,2048]{1,0:T(8,128)(2,1)S(1)}, u32[]{:S(2)}, u32[]{:S(2)}) collective-permute-start(bf16[256,2048]{1,0:T(8,128)(2,1)S(1)} %copy-done.1), channel_id=1, source_target_pairs={{0,16},{16,0},{1,17},{17,1},{2,18},{18,2},{3,19},{19,3},{4,20},{20... | collective-permute-start | bytes 3145736 | tf_op jit(solution)/shard_map/ppermute | solution.py:255
  62.0 1.9 collective-permute-start.2
  63.9 4.9 %collective-permute-start.4 = (bf16[2,128,896]{2,1,0:T(8,128)(2,1)}, bf16[2,128,896]{2,1,0:T(8,128)(2,1)S(1)}, u32[]{:S(2)}, u32[]{:S(2)}) collective-permute-start(bf16[2,128,896]{2,1,0:T(8,128)(2,1)} %param.8), channel_id=1, source_target_pairs={{30,0},{0,1},{16,2},{2,3},{18,4},{4,5},{20,6},{6,7},{22,8},{8,9},{... | collective-permute-start | bytes 1376264 | tf_op jit(solution)/shard_map/ppermute | solution.py:278
  68.9 3.3 %collective-permute-start = (bf16[384,1024]{1,0:T(8,128)(2,1)}, bf16[384,1024]{1,0:T(8,128)(2,1)}, u32[]{:S(2)}, u32[]{:S(2)}) collective-permute-start(bf16[384,1024]{1,0:T(8,128)(2,1)} %bitcast.10), channel_id=1, source_target_pairs={{0,16},{16,0},{1,17},{17,1},{2,18},{18,2},{3,19},{19,3},{4,20},{20... | collective-permute-start | bytes 2359304 | tf_op jit(solution)/shard_map/ppermute | solution.py:255
  72.2 2.6 %collective-permute-start.3 = (bf16[2,128,896]{2,1,0:T(8,128)(2,1)}, bf16[2,128,896]{2,1,0:T(8,128)(2,1)S(1)}, u32[]{:S(2)}, u32[]{:S(2)}) collective-permute-start(bf16[2,128,896]{2,1,0:T(8,128)(2,1)} %param.8), channel_id=1, source_target_pairs={{18,0},{2,1},{20,2},{4,3},{22,4},{6,5},{24,6},{8,7},{26,8},{10,9},... | collective-permute-start | bytes 1376264 | tf_op jit(solution)/shard_map/ppermute | solution.py:278
  74.9 9.0 %collective-permute-done.4.w1_ref = bf16[2,128,896]{2,1,0:T(8,128)(2,1)S(1)} collective-permute-done((bf16[2,128,896]{2,1,0:T(8,128)(2,1)}, bf16[2,128,896]{2,1,0:T(8,128)(2,1)S(1)}, u32[]{:S(2)}, u32[]{:S(2)}) %collective-permute-start.4) | collective-permute-done | bytes 458784 | tf_op jit(solution)/shard_map/ppermute | solution.py:278
  83.9 7.1 %collective-permute-start.5 = (bf16[2,128,896]{2,1,0:T(8,128)(2,1)}, bf16[2,128,896]{2,1,0:T(8,128)(2,1)S(1)}, u32[]{:S(2)}, u32[]{:S(2)}) collective-permute-start(bf16[2,128,896]{2,1,0:T(8,128)(2,1)} %param.8), channel_id=1, source_target_pairs={{0,0},{20,1},{2,2},{22,3},{4,4},{24,5},{6,6},{26,7},{8,8},{28,9},{... | collective-permute-start | bytes 1376264 | tf_op jit(solution)/shard_map/ppermute | solution.py:278
  91.0 11.3 %collective-permute-done.5.w2_ref = bf16[2,128,896]{2,1,0:T(8,128)(2,1)S(1)} collective-permute-done((bf16[2,128,896]{2,1,0:T(8,128)(2,1)}, bf16[2,128,896]{2,1,0:T(8,128)(2,1)S(1)}, u32[]{:S(2)}, u32[]{:S(2)}) %collective-permute-start.5) | collective-permute-done | bytes 458784 | tf_op jit(solution)/shard_map/ppermute | solution.py:278
  104.4 11.4 %near.1 = (bf16[256,2048]{1,0:T(8,128)(2,1)}, bf16[256,2048]{1,0:T(8,128)(2,1)}, bf16[16,3,8,896]{3,2,1,0:T(8,128)(2,1)}, bf16[768,896]{1,0:T(8,128)(2,1)}, bf16[768,128]{1,0:T(8,128)(2,1)}) custom-call(s32[1]{0:T(128)} %bitcast.place_ref, bf16[384,1024]{1,0:T(8,128)(2,1)} %bitcast.11, bf16[384,1024]{1,0:T(8,128)(2,1)} %collective-permute-done.other_ref, ...), custom_call_target="tpu_custom_call" | custom-call | tf_op jit(solution)/shard_map/near/pallas_call | solution.py:179
  115.8 6.9 %all-to-all-start.3 = ((bf16[16,3,8,896]{3,2,1,0:T(8,128)(2,1)}), bf16[16,3,8,896]{3,2,1,0:T(8,128)(2,1)S(1)}, u32[]{:S(2)}, u32[]{:S(2)}) async-start(bf16[16,3,8,896]{3,2,1,0:T(8,128)(2,1)} %get-tuple-element.22), calls=%async_computation.3 | async-start | bytes 1376256 | tf_op jit(solution)/shard_map/all_to_all | solution.py:259
  122.8 14.3 %far.1 = (bf16[256,2048]{1,0:T(8,128)(2,1)}, bf16[256,2048]{1,0:T(8,128)(2,1)}, bf16[16,5,8,896]{3,2,1,0:T(8,128)(2,1)}) custom-call(s32[1]{0:T(128)} %bitcast.place_ref, bf16[768,896]{1,0:T(8,128)(2,1)} %get-tuple-element.14.rows_ref, bf16[768,128]{1,0:T(8,128)(2,1)} %get-tuple-element.15.mask_ref, ...), custom_call_target="tpu_custom_call", output_to_operand_aliasing={{0}: (9, {}), {1}: (10, {})} | custom-call | tf_op jit(solution)/shard_map/far/pallas_call | solution.py:205
  137.1 6.8 %all-to-all-start.4 = ((bf16[16,5,8,896]{3,2,1,0:T(8,128)(2,1)}), bf16[16,5,8,896]{3,2,1,0:T(8,128)(2,1)S(1)}, u32[]{:S(2)}, u32[]{:S(2)}) async-start(bf16[16,5,8,896]{3,2,1,0:T(8,128)(2,1)} %get-tuple-element.23), calls=%async_computation.4 | async-start | bytes 2293760 | tf_op jit(solution)/shard_map/all_to_all | solution.py:259
  146.6 10.2 %all-to-all-done.4 = bf16[16,5,8,896]{3,2,1,0:T(8,128)(2,1)S(1)} async-done(((bf16[16,5,8,896]{3,2,1,0:T(8,128)(2,1)}), bf16[16,5,8,896]{3,2,1,0:T(8,128)(2,1)S(1)}, u32[]{:S(2)}, u32[]{:S(2)}) %all-to-all-start.4) | async-done | bytes 1146912 | tf_op jit(solution)/shard_map/all_to_all | solution.py:259
  159.2 7.2 %all-to-all-start.5 = ((bf16[16,8,896]{2,1,0:T(8,128)(2,1)}), bf16[16,8,896]{2,1,0:T(8,128)(2,1)S(1)}, u32[]{:S(2)}, u32[]{:S(2)}) async-start(bf16[16,8,896]{2,1,0:T(8,128)(2,1)} %arrange.1), calls=%async_computation.5 | async-start | bytes 458752 | tf_op jit(solution)/shard_map/all_to_all | solution.py:259
  166.4 2.7 %fusion.2 = bf16[256,2048]{1,0:T(8,128)(2,1)} fusion(bf16[256,2048]{1,0:T(8,128)(2,1)S(1)} %copy-done.4, bf16[256,2048]{1,0:T(8,128)(2,1)} %collective-permute-done.7, s32[]{:T(128)S(6)} %axis_index.51, s32[2048]{0:T(1024)S(1)} %get-tuple-element.26, s32[2048]{0:T(1024)S(1)} %get-tuple-element.27, pred[2048]{0:T(1024)(128)(4,1)S(1)} %fusion.5), kind=kLoop, calls=%fused_computation.7 | loop fusion | flops 7340032 | bytes 3164164 | tf_op jit(solution)/shard_map/jit(_where)/select_n | solution.py:308
  169.2 9.7 %all-to-all-done.5 = bf16[16,8,896]{2,1,0:T(8,128)(2,1)S(1)} async-done(((bf16[16,8,896]{2,1,0:T(8,128)(2,1)}), bf16[16,8,896]{2,1,0:T(8,128)(2,1)S(1)}, u32[]{:S(2)}, u32[]{:S(2)}) %all-to-all-start.5) | async-done | bytes 229408 | tf_op jit(solution)/shard_map/all_to_all | solution.py:259
  179.8 9.8 %all-to-all-start.6 = ((bf16[32,8,896]{2,1,0:T(8,128)(2,1)}), bf16[32,8,896]{2,1,0:T(8,128)(2,1)S(1)}, u32[]{:S(2)}, u32[]{:S(2)}) async-start(bf16[32,8,896]{2,1,0:T(8,128)(2,1)} %broadcast_in_dim.22), calls=%async_computation.6 | async-start | bytes 917504 | tf_op jit(solution)/shard_map/all_to_all | solution.py:259
  189.6 10.9 %all-to-all-done.6 = bf16[32,8,896]{2,1,0:T(8,128)(2,1)S(1)} async-done(((bf16[32,8,896]{2,1,0:T(8,128)(2,1)}), bf16[32,8,896]{2,1,0:T(8,128)(2,1)S(1)}, u32[]{:S(2)}, u32[]{:S(2)}) %all-to-all-start.6) | async-done | bytes 458784 | tf_op jit(solution)/shard_map/all_to_all | solution.py:259
  (44 shorter events, 15.4 us)
Async XLA Ops:
  2.1 28.4 %all-to-all-start.1 = ((bf16[16,8,896]{2,1,0:T(8,128)(2,1)}), bf16[16,8,896]{2,1,0:T(8,128)(2,1)S(1)}, u32[]{:S(2)}, u32[]{:S(2)}) async-start(bf16[16,8,896]{2,1,0:T(8,128)(2,1)} %broadcast_in_dim.9), calls=%async_computation.1 | async-start | bytes 458752 | tf_op jit(solution)/shard_map/all_to_all | solution.py:259
  30.5 6.8 %copy-start.6 = (bf16[16,8,896]{2,1,0:T(8,128)(2,1)}, bf16[16,8,896]{2,1,0:T(8,128)(2,1)S(1)}, u32[]{:S(2)}) copy-start(bf16[16,8,896]{2,1,0:T(8,128)(2,1)S(1)} %all-to-all-done.1.heads_ref) | copy-start | bytes 688132
  30.5 18.0 %all-to-all-start = ((bf16[16,24,1024]{2,1,0:T(8,128)(2,1)}), bf16[16,24,1024]{2,1,0:T(8,128)(2,1)S(1)}, u32[]{:S(2)}, u32[]{:S(2)}) async-start(bf16[16,24,1024]{2,1,0:T(8,128)(2,1)} %bitcast.12), calls=%async_computation | async-start | bytes 1572864 | tf_op jit(solution)/shard_map/all_to_all | solution.py:259
  38.9 8.7 %collective-permute-start.6 = (bf16[5,8,896]{2,1,0:T(8,128)(2,1)}, bf16[5,8,896]{2,1,0:T(8,128)(2,1)S(1)}, u32[]{:S(2)}, u32[]{:S(2)}) collective-permute-start(bf16[5,8,896]{2,1,0:T(8,128)(2,1)} %get-tuple-element.17), channel_id=1, source_target_pairs={{0,16},{16,0},{1,17},{17,1},{2,18},{18,2},{3,19},{19,3},{4,20},{20... | collective-permute-start | bytes 215048 | tf_op jit(solution)/shard_map/ppermute | solution.py:255
  48.5 1.7 copy-start.5
  50.2 7.1 %copy-start.1 = (bf16[256,2048]{1,0:T(8,128)(2,1)S(1)}, bf16[256,2048]{1,0:T(8,128)(2,1)}, u32[]{:S(2)}) copy-start(bf16[256,2048]{1,0:T(8,128)(2,1)} %q_ref.3) | copy-start | bytes 3145732
  50.2 65.6 %all-to-all-start.2 = ((bf16[16,2,5,8,896]{4,3,2,1,0:T(8,128)(2,1)}), bf16[16,2,5,8,896]{4,3,2,1,0:T(8,128)(2,1)S(1)}, u32[]{:S(2)}, u32[]{:S(2)}) async-start(bf16[16,2,5,8,896]{4,3,2,1,0:T(8,128)(2,1)} %broadcast_in_dim.10), calls=%async_computation.2 | async-start | bytes 4587520 | tf_op jit(solution)/shard_map/all_to_all | solution.py:259
  57.3 45.0 %collective-permute-start.1 = (bf16[256,2048]{1,0:T(8,128)(2,1)S(1)}, bf16[256,2048]{1,0:T(8,128)(2,1)S(1)}, u32[]{:S(2)}, u32[]{:S(2)}) collective-permute-start(bf16[256,2048]{1,0:T(8,128)(2,1)S(1)} %copy-done.1), channel_id=1, source_target_pairs={{0,16},{16,0},{1,17},{17,1},{2,18},{18,2},{3,19},{19,3},{4,20},{20... | collective-permute-start | bytes 3145736 | tf_op jit(solution)/shard_map/ppermute | solution.py:255
  62.0 41.3 %collective-permute-start.2 = (bf16[256,2048]{1,0:T(8,128)(2,1)}, bf16[256,2048]{1,0:T(8,128)(2,1)S(1)}, u32[]{:S(2)}, u32[]{:S(2)}) collective-permute-start(bf16[256,2048]{1,0:T(8,128)(2,1)} %g_ref.3), channel_id=1, source_target_pairs={{0,16},{16,0},{1,17},{17,1},{2,18},{18,2},{3,19},{19,3},{4,20},{20... | collective-permute-start | bytes 3145736 | tf_op jit(solution)/shard_map/ppermute | solution.py:255
  63.9 19.9 %collective-permute-start.4 = (bf16[2,128,896]{2,1,0:T(8,128)(2,1)}, bf16[2,128,896]{2,1,0:T(8,128)(2,1)S(1)}, u32[]{:S(2)}, u32[]{:S(2)}) collective-permute-start(bf16[2,128,896]{2,1,0:T(8,128)(2,1)} %param.8), channel_id=1, source_target_pairs={{30,0},{0,1},{16,2},{2,3},{18,4},{4,5},{20,6},{6,7},{22,8},{8,9},{... | collective-permute-start | bytes 1376264 | tf_op jit(solution)/shard_map/ppermute | solution.py:278
  68.9 35.5 %collective-permute-start = (bf16[384,1024]{1,0:T(8,128)(2,1)}, bf16[384,1024]{1,0:T(8,128)(2,1)}, u32[]{:S(2)}, u32[]{:S(2)}) collective-permute-start(bf16[384,1024]{1,0:T(8,128)(2,1)} %bitcast.10), channel_id=1, source_target_pairs={{0,16},{16,0},{1,17},{17,1},{2,18},{18,2},{3,19},{19,3},{4,20},{20... | collective-permute-start | bytes 2359304 | tf_op jit(solution)/shard_map/ppermute | solution.py:255
  72.2 18.8 %collective-permute-start.3 = (bf16[2,128,896]{2,1,0:T(8,128)(2,1)}, bf16[2,128,896]{2,1,0:T(8,128)(2,1)S(1)}, u32[]{:S(2)}, u32[]{:S(2)}) collective-permute-start(bf16[2,128,896]{2,1,0:T(8,128)(2,1)} %param.8), channel_id=1, source_target_pairs={{18,0},{2,1},{20,2},{4,3},{22,4},{6,5},{24,6},{8,7},{26,8},{10,9},... | collective-permute-start | bytes 1376264 | tf_op jit(solution)/shard_map/ppermute | solution.py:278
  83.9 19.4 %copy-start.7 = (bf16[2,128,896]{2,1,0:T(8,128)(2,1)}, bf16[2,128,896]{2,1,0:T(8,128)(2,1)S(1)}, u32[]{:S(2)}) copy-start(bf16[2,128,896]{2,1,0:T(8,128)(2,1)S(1)} %collective-permute-done.4.w1_ref) | copy-start | bytes 1376260
  83.9 18.4 %collective-permute-start.5 = (bf16[2,128,896]{2,1,0:T(8,128)(2,1)}, bf16[2,128,896]{2,1,0:T(8,128)(2,1)S(1)}, u32[]{:S(2)}, u32[]{:S(2)}) collective-permute-start(bf16[2,128,896]{2,1,0:T(8,128)(2,1)} %param.8), channel_id=1, source_target_pairs={{0,0},{20,1},{2,2},{22,3},{4,4},{24,5},{6,6},{26,7},{8,8},{28,9},{... | collective-permute-start | bytes 1376264 | tf_op jit(solution)/shard_map/ppermute | solution.py:278
  91.0 12.3 %copy-start.8 = (bf16[2,128,896]{2,1,0:T(8,128)(2,1)}, bf16[2,128,896]{2,1,0:T(8,128)(2,1)S(1)}, u32[]{:S(2)}) copy-start(bf16[2,128,896]{2,1,0:T(8,128)(2,1)S(1)} %collective-permute-done.3.w0_ref) | copy-start | bytes 1376260
  102.3 1.1 copy-start.9
  102.3 1.0 copy-start.2
  115.8 6.9 %copy-start = (bf16[16,2,5,8,896]{4,3,2,1,0:T(8,128)(2,1)}, bf16[16,2,5,8,896]{4,3,2,1,0:T(8,128)(2,1)S(1)}, u32[]{:S(2)}) copy-start(bf16[16,2,5,8,896]{4,3,2,1,0:T(8,128)(2,1)S(1)} %all-to-all-done.2.wk_ref.wv_ref) | copy-start | bytes 6881284
  115.8 21.2 %all-to-all-start.3 = ((bf16[16,3,8,896]{3,2,1,0:T(8,128)(2,1)}), bf16[16,3,8,896]{3,2,1,0:T(8,128)(2,1)S(1)}, u32[]{:S(2)}, u32[]{:S(2)}) async-start(bf16[16,3,8,896]{3,2,1,0:T(8,128)(2,1)} %get-tuple-element.22), calls=%async_computation.3 | async-start | bytes 1376256 | tf_op jit(solution)/shard_map/all_to_all | solution.py:259
  137.1 29.3 %copy-start.4 = (bf16[256,2048]{1,0:T(8,128)(2,1)S(1)}, bf16[256,2048]{1,0:T(8,128)(2,1)}, u32[]{:S(2)}) copy-start(bf16[256,2048]{1,0:T(8,128)(2,1)} %get-tuple-element.20) | copy-start | bytes 3145732
  137.1 19.7 %all-to-all-start.4 = ((bf16[16,5,8,896]{3,2,1,0:T(8,128)(2,1)}), bf16[16,5,8,896]{3,2,1,0:T(8,128)(2,1)S(1)}, u32[]{:S(2)}, u32[]{:S(2)}) async-start(bf16[16,5,8,896]{3,2,1,0:T(8,128)(2,1)} %get-tuple-element.23), calls=%async_computation.4 | async-start | bytes 2293760 | tf_op jit(solution)/shard_map/all_to_all | solution.py:259
  143.9 22.5 %collective-permute-start.7 = (bf16[256,2048]{1,0:T(8,128)(2,1)}, bf16[256,2048]{1,0:T(8,128)(2,1)}, u32[]{:S(2)}, u32[]{:S(2)}) collective-permute-start(bf16[256,2048]{1,0:T(8,128)(2,1)} %get-tuple-element.21), channel_id=1, source_target_pairs={{0,16},{16,0},{1,17},{17,1},{2,18},{18,2},{3,19},{19,3},{4,20},{20... | collective-permute-start | bytes 3145736 | tf_op jit(solution)/shard_map/ppermute | solution.py:255
  159.2 19.7 %all-to-all-start.5 = ((bf16[16,8,896]{2,1,0:T(8,128)(2,1)}), bf16[16,8,896]{2,1,0:T(8,128)(2,1)S(1)}, u32[]{:S(2)}, u32[]{:S(2)}) async-start(bf16[16,8,896]{2,1,0:T(8,128)(2,1)} %arrange.1), calls=%async_computation.5 | async-start | bytes 458752 | tf_op jit(solution)/shard_map/all_to_all | solution.py:259
  179.8 20.7 %all-to-all-start.6 = ((bf16[32,8,896]{2,1,0:T(8,128)(2,1)}), bf16[32,8,896]{2,1,0:T(8,128)(2,1)S(1)}, u32[]{:S(2)}, u32[]{:S(2)}) async-start(bf16[32,8,896]{2,1,0:T(8,128)(2,1)} %broadcast_in_dim.22), calls=%async_computation.6 | async-start | bytes 917504 | tf_op jit(solution)/shard_map/all_to_all | solution.py:259
  (1 other events, 1.0 us)
where the time goes:
time: 202 us; the launch traced here: 201 us
  starting transfers between devices  94.4 us (47%)
  waiting for transfers between devices  61.5 us (30%)
  Pallas kernels  31.8 us (16%)
  local copies, waits for them, and re-layouts  6.71 us (3%)
  other arithmetic  5.18 us (3%)
    all_to_all x7, starting transfers between devices, exchange(): return lax.all_to_all(array, axis, split_axis=0, concat_axis=0, tiled=True)  60.2 us
    all_to_all x7, waiting for transfers between devices, exchange(): return lax.all_to_all(array, axis, split_axis=0, concat_axis=0, tiled=True)  40.1 us
    ppermute x3, waiting for transfers between devices, fetch(): return lax.ppermute(array, ('c', 'z'), pairs)  20.3 us
    ppermute x5, starting transfers between devices, swap(): return lax.ppermute(array, 'c', [(0, 1), (1, 0)])  19.5 us
    ppermute x3, starting transfers between devices, fetch(): return lax.ppermute(array, ('c', 'z'), pairs)  14.7 us
    pallas_call x1, Pallas kernels, attend_far(): pl.pallas_call(far_body, grid_spec=pltpu.PrefetchScalarGridSpec(num_scala...  14.3 us
    pallas_call x1, Pallas kernels, attend_near(): pl.pallas_call(near_body, grid_spec=pltpu.PrefetchScalarGridSpec(num_scal...  11.4 us
  transfers between devices with their start and end apart: 15, of which 7 were waited for; matrix products, arithmetic and copies ran while one was open for 3% of the time, Pallas kernels for 16%

commit v1 on v0

--- a/solution.py
+++ b/solution.py
@@ -15,6 +15,7 @@
 DP = 32
 CAP = 12
 PLANE = 16
+HALF = HEADS // 2
 EXT = ENC + 128
 BIG = 2.0**100
 SCALE = 1.0 / HEAD_DIM**0.5
@@ -79,9 +80,9 @@
     return (z + turn) & (HEADS - 1)
 
 
-def attend_step(rows_ref, mask_ref, q_ref, g_ref, q2_ref, g2_ref, w_ref, gq_ref, gq2_ref, part_ref, dval_ref):
+def attend_step(rows_ref, mask_ref, q_ref, g_ref, q2_ref, g2_ref, w_ref, gq_ref, gq2_ref, part_ref, dval_ref, first=0):
     step = pl.program_id(0)
-    group = part_ref.shape[1]
+    group = part_ref.shape[1] - first
     rows = rows_ref[...]
     pair = dot(rows, w_ref[...], NT).astype(jnp.bfloat16)
     token = lax.broadcasted_iota(jnp.int32, (TOK, 128), 0)
@@ -108,7 +109,7 @@
         partial = dot(dval_ref[...], rows, NN)
         for j in range(group):
             block = partial[j * HEAD_DIM : (j + 1) * HEAD_DIM]
-            part_ref[:, j, :, :] = block.reshape(PLANE, 8, ENC).astype(jnp.bfloat16)
+            part_ref[:, first + j, :, :] = block.reshape(PLANE, 8, ENC).astype(jnp.bfloat16)
 
 
 def near_body(
@@ -146,12 +147,17 @@
 
 
 def far_body(
-    place_ref, rows_ref, mask_ref, q_ref, g_ref, q2_ref, g2_ref, wk_ref, wv_ref, a0, a1,
+    place_ref, rows_ref, mask_ref, q_ref, g_ref, q2_ref, g2_ref, wk_ref, wv_ref, near_ref, a0, a1,
     gq_ref, gq2_ref, part_ref, w_ref, dval_ref,
 ):
     w_ref[:HEAD_DIM, :] = wk_ref[...].reshape(HEAD_DIM, ENC)
     w_ref[HEAD_DIM:, :] = wv_ref[...].reshape(HEAD_DIM, ENC)
-    attend_step(rows_ref, mask_ref, q_ref, g_ref, q2_ref, g2_ref, w_ref, gq_ref, gq2_ref, part_ref, dval_ref)
+    first = near_ref.shape[1]
+    attend_step(rows_ref, mask_ref, q_ref, g_ref, q2_ref, g2_ref, w_ref, gq_ref, gq2_ref, part_ref, dval_ref, first)
+
+    @pl.when(pl.program_id(0) == 0)
+    def _():
+        part_ref[:, :first] = near_ref[...]
 
 
 WIDE = jax.ShapeDtypeStruct((TOK, HEADS * HEAD_DIM), jnp.bfloat16)
@@ -197,7 +203,7 @@
     )(place, own, other, *tokens, *weights)
 
 
-def attend_far(place, rows, mask, tokens, weights, gq, gq2, interpret=False):
+def attend_far(place, rows, mask, tokens, weights, near, gq, gq2, interpret=False):
     head = head_block(FAR)
     group = weights.shape[2]
     kv = lambda pick: pl.BlockSpec((PLANE, 1, 1, 8, ENC), lambda i, place: (0, pick(place[0] >> 4), i, 0, 0))
@@ -210,15 +216,16 @@
             in_specs=[whole(2 * ROWS, ENC), whole(2 * ROWS, 128)]
             + [head] * 4
             + [kv(lambda c: c), kv(lambda c: 1 - c)]
+            + [whole(*near.shape)]
             + [kept] * 2,
-            out_specs=[head, head, whole(PLANE, group, 8, ENC)],
+            out_specs=[head, head, whole(PLANE, HALF, 8, ENC)],
             scratch_shapes=work(group),
         ),
-        out_shape=[WIDE, WIDE, part_of(group)],
-        input_output_aliases={9: 0, 10: 1},
+        out_shape=[WIDE, WIDE, part_of(HALF)],
+        input_output_aliases={10: 0, 11: 1},
         interpret=interpret,
         name="far",
-    )(place, rows, mask, *tokens, weights, weights, gq, gq2)
+    )(place, rows, mask, *tokens, weights, weights, near, gq, gq2)
 
 
 def deal_body(place_ref, heads_ref, kept_ref, given_ref):
@@ -238,17 +245,17 @@
     )(place, heads)
 
 
-def arrange_body(place_ref, near_ref, far_ref, out_ref):
-    for ref, offsets in ((near_ref, NEAR), (far_ref, FAR)):
-        for i in range(len(offsets[0])):
-            out_ref[head_of(i, place_ref, offsets)] = ref[i]
-
-
-def arrange(place, near, far, interpret=False):
+def arrange_body(place_ref, sums_ref, out_ref):
+    both = tuple(n + f for n, f in zip(NEAR, FAR))
+    for i in range(HALF):
+        out_ref[head_of(i, place_ref, both)] = sums_ref[i]
+
+
+def arrange(place, sums, interpret=False):
     shape = jax.ShapeDtypeStruct((HEADS, 8, ENC), jnp.bfloat16)
     return pl.pallas_call(
-        arrange_body, out_shape=shape, in_specs=[SMEM, VMEM, VMEM], out_specs=VMEM, interpret=interpret, name="arrange"
-    )(place, near, far)
+        arrange_body, out_shape=shape, in_specs=[SMEM, VMEM], out_specs=VMEM, interpret=interpret, name="arrange"
+    )(place, sums)
 
 
 def swap(array):
@@ -298,11 +305,8 @@
     tokens = (queries, grad_ctx, swap(queries), swap(grad_ctx))
 
     gq, gq2, part, rows, mask = attend_near(place, arrived, other, tokens, near)
-    near_part = exchange(part, ("y", "x"))
-    gq, gq2, part = attend_far(place, rows, mask, tokens, weights, gq, gq2)
-    far_part = exchange(part, ("y", "x"))
-
-    sums = arrange(place, *(total(part).astype(jnp.bfloat16) for part in (near_part, far_part)))
+    gq, gq2, part = attend_far(place, rows, mask, tokens, weights, part, gq, gq2)
+    sums = arrange(place, total(exchange(part, ("y", "x"))).astype(jnp.bfloat16))
     final = (total(exchange(sums, "z")) / DP).astype(jnp.bfloat16)
     own_head = (lax.broadcasted_iota(jnp.int32, gq.shape, 1) // HEAD_DIM) % 2 == c
     grad_queries, final = lax.optimization_barrier((jnp.where(own_head, gq, swap(gq2)), final))

time: 202 us -> 203 us (level)
  starting transfers between devices: 94.4 us -> 84 us
  waiting for transfers between devices: 61.5 us -> 71.6 us
    all_to_all x7 -> x6, waiting for transfers between devices: 40.1 us -> 49.3 us  [exchange(): return lax.all_to_all(array, axis, split_axis=0, concat_axis=0, tiled=True)]
    all_to_all x7 -> x6, starting transfers between devices: 60.2 us -> 52.5 us  [exchange(): return lax.all_to_all(array, axis, split_axis=0, concat_axis=0, tiled=True)]
  transfers between devices with their start and end apart: 15 -> 14, of which waited for: 7 -> 8; matrix products, arithmetic and copies ran while one was open for 3% -> 2% of each run, Pallas kernels for 16% -> 9%
where the time goes in v1:
time: 203 us; the launch traced here: 202 us
  starting transfers between devices  84 us (41%)
  waiting for transfers between devices  71.6 us (35%)
  Pallas kernels  32.2 us (16%)
  local copies, waits for them, and re-layouts  8.27 us (4%)
  other arithmetic  4.58 us (2%)
    all_to_all x6, starting transfers between devices, exchange(): return lax.all_to_all(array, axis, split_axis=0, concat_axis=0, tiled=True)  52.5 us
    all_to_all x6, waiting for transfers between devices, exchange(): return lax.all_to_all(array, axis, split_axis=0, concat_axis=0, tiled=True)  49.3 us
    ppermute x3, waiting for transfers between devices, fetch(): return lax.ppermute(array, ('c', 'z'), pairs)  21.2 us
    ppermute x5, starting transfers between devices, swap(): return lax.ppermute(array, 'c', [(0, 1), (1, 0)])  18.3 us
    pallas_call x1, Pallas kernels, attend_far(): pl.pallas_call(far_body, grid_spec=pltpu.PrefetchScalarGridSpec(num_scala...  14.8 us
    ppermute x3, starting transfers between devices, fetch(): return lax.ppermute(array, ('c', 'z'), pairs)  13.2 us
    pallas_call x1, Pallas kernels, attend_near(): pl.pallas_call(near_body, grid_spec=pltpu.PrefetchScalarGridSpec(num_scal...  11.4 us
  transfers between devices with their start and end apart: 14, of which 8 were waited for; matrix products, arithmetic and copies ran while one was open for 2% of the time, Pallas kernels for 9%

profile of v1, /device:TPU:1, one launch (start us, length us, event | category | flops | bytes accessed | tf_op | source)
XLA Modules:
  0.0 202.2 jit_solution(5767195147004524814)
XLA Ops:
  2.1 15.7 %all-to-all-start.1 = ((bf16[16,8,896]{2,1,0:T(8,128)(2,1)}), bf16[16,8,896]{2,1,0:T(8,128)(2,1)S(1)}, u32[]{:S(2)}, u32[]{:S(2)}) async-start(bf16[16,8,896]{2,1,0:T(8,128)(2,1)} %broadcast_in_dim.9), calls=%async_computation.1 | async-start | bytes 458752 | tf_op jit(solution)/shard_map/all_to_all | solution.py:266
  18.5 2.8 %pack.1 = bf16[384,1024]{1,0:T(8,128)(2,1)} custom-call(s32[1]{0:T(128)S(6)} %copy.13.count_ref, s32[384]{0:T(512)} %rank_ref.1, s32[384]{0:T(512)} %span_ref.1, bf16[384,896]{1,0:T(8,128)(2,1)} %enc_ref.1), custom_call_target="tpu_custom_call" | custom-call | tf_op jit(solution)/shard_map/pack/pallas_call | solution.py:51
  21.2 9.2 %all-to-all-done.1.heads_ref = bf16[16,8,896]{2,1,0:T(8,128)(2,1)S(1)} async-done(((bf16[16,8,896]{2,1,0:T(8,128)(2,1)}), bf16[16,8,896]{2,1,0:T(8,128)(2,1)S(1)}, u32[]{:S(2)}, u32[]{:S(2)}) %all-to-all-start.1) | async-done | bytes 229408 | tf_op jit(solution)/shard_map/all_to_all | solution.py:266
  30.5 6.8 %all-to-all-start = ((bf16[16,24,1024]{2,1,0:T(8,128)(2,1)}), bf16[16,24,1024]{2,1,0:T(8,128)(2,1)S(1)}, u32[]{:S(2)}, u32[]{:S(2)}) async-start(bf16[16,24,1024]{2,1,0:T(8,128)(2,1)} %bitcast.12), calls=%async_computation | async-start | bytes 1572864 | tf_op jit(solution)/shard_map/all_to_all | solution.py:266
  38.9 7.6 %collective-permute-start.6 = (bf16[5,8,896]{2,1,0:T(8,128)(2,1)}, bf16[5,8,896]{2,1,0:T(8,128)(2,1)S(1)}, u32[]{:S(2)}, u32[]{:S(2)}) collective-permute-start(bf16[5,8,896]{2,1,0:T(8,128)(2,1)} %get-tuple-element.17), channel_id=1, source_target_pairs={{0,16},{16,0},{1,17},{17,1},{2,18},{18,2},{3,19},{19,3},{4,20},{20... | collective-permute-start | bytes 215048 | tf_op jit(solution)/shard_map/ppermute | solution.py:262
  50.3 7.1 %all-to-all-start.2 = ((bf16[16,2,5,8,896]{4,3,2,1,0:T(8,128)(2,1)}), bf16[16,2,5,8,896]{4,3,2,1,0:T(8,128)(2,1)S(1)}, u32[]{:S(2)}, u32[]{:S(2)}) async-start(bf16[16,2,5,8,896]{4,3,2,1,0:T(8,128)(2,1)} %broadcast_in_dim.10), calls=%async_computation.2 | async-start | bytes 4587520 | tf_op jit(solution)/shard_map/all_to_all | solution.py:266
  57.3 4.7 %collective-permute-start.1 = (bf16[256,2048]{1,0:T(8,128)(2,1)S(1)}, bf16[256,2048]{1,0:T(8,128)(2,1)S(1)}, u32[]{:S(2)}, u32[]{:S(2)}) collective-permute-start(bf16[256,2048]{1,0:T(8,128)(2,1)S(1)} %copy-done.1), channel_id=1, source_target_pairs={{0,16},{16,0},{1,17},{17,1},{2,18},{18,2},{3,19},{19,3},{4,20},{20... | collective-permute-start | bytes 3145736 | tf_op jit(solution)/shard_map/ppermute | solution.py:262
  62.1 1.9 collective-permute-start.2
  64.0 6.3 %collective-permute-start.3 = (bf16[2,128,896]{2,1,0:T(8,128)(2,1)}, bf16[2,128,896]{2,1,0:T(8,128)(2,1)S(1)}, u32[]{:S(2)}, u32[]{:S(2)}) collective-permute-start(bf16[2,128,896]{2,1,0:T(8,128)(2,1)} %param.8), channel_id=1, source_target_pairs={{18,0},{2,1},{20,2},{4,3},{22,4},{6,5},{24,6},{8,7},{26,8},{10,9},... | collective-permute-start | bytes 1376264 | tf_op jit(solution)/shard_map/ppermute | solution.py:285
  70.3 1.9 collective-permute-start
  72.2 3.1 %collective-permute-start.4 = (bf16[2,128,896]{2,1,0:T(8,128)(2,1)}, bf16[2,128,896]{2,1,0:T(8,128)(2,1)S(1)}, u32[]{:S(2)}, u32[]{:S(2)}) collective-permute-start(bf16[2,128,896]{2,1,0:T(8,128)(2,1)} %param.8), channel_id=1, source_target_pairs={{30,0},{0,1},{16,2},{2,3},{18,4},{4,5},{20,6},{6,7},{22,8},{8,9},{... | collective-permute-start | bytes 1376264 | tf_op jit(solution)/shard_map/ppermute | solution.py:285
  75.3 10.4 %collective-permute-done.3.w0_ref = bf16[2,128,896]{2,1,0:T(8,128)(2,1)S(1)} collective-permute-done((bf16[2,128,896]{2,1,0:T(8,128)(2,1)}, bf16[2,128,896]{2,1,0:T(8,128)(2,1)S(1)}, u32[]{:S(2)}, u32[]{:S(2)}) %collective-permute-start.3) | collective-permute-done | bytes 458784 | tf_op jit(solution)/shard_map/ppermute | solution.py:285
  85.7 3.9 %collective-permute-start.5 = (bf16[2,128,896]{2,1,0:T(8,128)(2,1)}, bf16[2,128,896]{2,1,0:T(8,128)(2,1)S(1)}, u32[]{:S(2)}, u32[]{:S(2)}) collective-permute-start(bf16[2,128,896]{2,1,0:T(8,128)(2,1)} %param.8), channel_id=1, source_target_pairs={{0,0},{20,1},{2,2},{22,3},{4,4},{24,5},{6,6},{26,7},{8,8},{28,9},{... | collective-permute-start | bytes 1376264 | tf_op jit(solution)/shard_map/ppermute | solution.py:285
  91.4 8.9 %collective-permute-done.5.w2_ref = bf16[2,128,896]{2,1,0:T(8,128)(2,1)S(1)} collective-permute-done((bf16[2,128,896]{2,1,0:T(8,128)(2,1)}, bf16[2,128,896]{2,1,0:T(8,128)(2,1)S(1)}, u32[]{:S(2)}, u32[]{:S(2)}) %collective-permute-start.5) | collective-permute-done | bytes 458784 | tf_op jit(solution)/shard_map/ppermute | solution.py:285
  102.5 11.4 %near.1 = (bf16[256,2048]{1,0:T(8,128)(2,1)}, bf16[256,2048]{1,0:T(8,128)(2,1)}, bf16[16,3,8,896]{3,2,1,0:T(8,128)(2,1)}, bf16[768,896]{1,0:T(8,128)(2,1)}, bf16[768,128]{1,0:T(8,128)(2,1)}) custom-call(s32[1]{0:T(128)} %bitcast.place_ref, bf16[384,1024]{1,0:T(8,128)(2,1)} %bitcast.11, bf16[384,1024]{1,0:T(8,128)(2,1)} %collective-permute-done.other_ref, ...), custom_call_target="tpu_custom_call" | custom-call | tf_op jit(solution)/shard_map/near/pallas_call | solution.py:185
  115.4 14.8 %far.1 = (bf16[256,2048]{1,0:T(8,128)(2,1)}, bf16[256,2048]{1,0:T(8,128)(2,1)}, bf16[16,8,8,896]{3,2,1,0:T(8,128)(2,1)}) custom-call(s32[1]{0:T(128)} %bitcast.place_ref, bf16[768,896]{1,0:T(8,128)(2,1)} %get-tuple-element.14.rows_ref, bf16[768,128]{1,0:T(8,128)(2,1)} %get-tuple-element.15.mask_ref, ...), custom_call_target="tpu_custom_call", output_to_operand_aliasing={{0}: (10, {}), {1}: (11, {})} | custom-call | tf_op jit(solution)/shard_map/far/pallas_call | solution.py:211
  130.2 6.9 %all-to-all-start.3 = ((bf16[16,8,8,896]{3,2,1,0:T(8,128)(2,1)}), bf16[16,8,8,896]{3,2,1,0:T(8,128)(2,1)S(1)}, u32[]{:S(2)}, u32[]{:S(2)}) async-start(bf16[16,8,8,896]{3,2,1,0:T(8,128)(2,1)} %get-tuple-element.23), calls=%async_computation.3 | async-start | bytes 3670016 | tf_op jit(solution)/shard_map/all_to_all | solution.py:266
  137.1 2.1 %collective-permute-start.7 = (bf16[256,2048]{1,0:T(8,128)(2,1)}, bf16[256,2048]{1,0:T(8,128)(2,1)}, u32[]{:S(2)}, u32[]{:S(2)}) collective-permute-start(bf16[256,2048]{1,0:T(8,128)(2,1)} %get-tuple-element.22), channel_id=1, source_target_pairs={{0,16},{16,0},{1,17},{17,1},{2,18},{18,2},{3,19},{19,3},{4,20},{20... | collective-permute-start | bytes 3145736 | tf_op jit(solution)/shard_map/ppermute | solution.py:262
  139.1 19.4 %all-to-all-done.3 = bf16[16,8,8,896]{3,2,1,0:T(8,128)(2,1)S(1)} async-done(((bf16[16,8,8,896]{3,2,1,0:T(8,128)(2,1)}), bf16[16,8,8,896]{3,2,1,0:T(8,128)(2,1)S(1)}, u32[]{:S(2)}, u32[]{:S(2)}) %all-to-all-start.3) | async-done | bytes 1835040 | tf_op jit(solution)/shard_map/all_to_all | solution.py:266
  161.1 6.3 %all-to-all-start.4 = ((bf16[16,8,896]{2,1,0:T(8,128)(2,1)}), bf16[16,8,896]{2,1,0:T(8,128)(2,1)S(1)}, u32[]{:S(2)}, u32[]{:S(2)}) async-start(bf16[16,8,896]{2,1,0:T(8,128)(2,1)} %arrange.1), calls=%async_computation.4 | async-start | bytes 458752 | tf_op jit(solution)/shard_map/all_to_all | solution.py:266
  167.4 2.7 %fusion.2 = bf16[256,2048]{1,0:T(8,128)(2,1)} fusion(bf16[256,2048]{1,0:T(8,128)(2,1)S(1)} %copy-done.4, bf16[256,2048]{1,0:T(8,128)(2,1)} %collective-permute-done.7, s32[]{:T(128)S(6)} %axis_index.51, s32[2048]{0:T(1024)S(1)} %get-tuple-element.26, s32[2048]{0:T(1024)S(1)} %get-tuple-element.27, pred[2048]{0:T(1024)(128)(4,1)S(1)} %fusion.5), kind=kLoop, calls=%fused_computation.7 | loop fusion | flops 7340032 | bytes 3164164 | tf_op jit(solution)/shard_map/jit(_where)/select_n | solution.py:312
  170.1 9.7 %all-to-all-done.4 = bf16[16,8,896]{2,1,0:T(8,128)(2,1)S(1)} async-done(((bf16[16,8,896]{2,1,0:T(8,128)(2,1)}), bf16[16,8,896]{2,1,0:T(8,128)(2,1)S(1)}, u32[]{:S(2)}, u32[]{:S(2)}) %all-to-all-start.4) | async-done | bytes 229408 | tf_op jit(solution)/shard_map/all_to_all | solution.py:266
  180.8 9.8 %all-to-all-start.5 = ((bf16[32,8,896]{2,1,0:T(8,128)(2,1)}), bf16[32,8,896]{2,1,0:T(8,128)(2,1)S(1)}, u32[]{:S(2)}, u32[]{:S(2)}) async-start(bf16[32,8,896]{2,1,0:T(8,128)(2,1)} %broadcast_in_dim.22), calls=%async_computation.5 | async-start | bytes 917504 | tf_op jit(solution)/shard_map/all_to_all | solution.py:266
  190.6 10.9 %all-to-all-done.5 = bf16[32,8,896]{2,1,0:T(8,128)(2,1)S(1)} async-done(((bf16[32,8,896]{2,1,0:T(8,128)(2,1)}), bf16[32,8,896]{2,1,0:T(8,128)(2,1)S(1)}, u32[]{:S(2)}, u32[]{:S(2)}) %all-to-all-start.5) | async-done | bytes 458784 | tf_op jit(solution)/shard_map/all_to_all | solution.py:266
  (41 shorter events, 16.3 us)
Async XLA Ops:
  2.1 28.4 %all-to-all-start.1 = ((bf16[16,8,896]{2,1,0:T(8,128)(2,1)}), bf16[16,8,896]{2,1,0:T(8,128)(2,1)S(1)}, u32[]{:S(2)}, u32[]{:S(2)}) async-start(bf16[16,8,896]{2,1,0:T(8,128)(2,1)} %broadcast_in_dim.9), calls=%async_computation.1 | async-start | bytes 458752 | tf_op jit(solution)/shard_map/all_to_all | solution.py:266
  30.5 6.8 %copy-start.6 = (bf16[16,8,896]{2,1,0:T(8,128)(2,1)}, bf16[16,8,896]{2,1,0:T(8,128)(2,1)S(1)}, u32[]{:S(2)}) copy-start(bf16[16,8,896]{2,1,0:T(8,128)(2,1)S(1)} %all-to-all-done.1.heads_ref) | copy-start | bytes 688132
  30.5 18.0 %all-to-all-start = ((bf16[16,24,1024]{2,1,0:T(8,128)(2,1)}), bf16[16,24,1024]{2,1,0:T(8,128)(2,1)S(1)}, u32[]{:S(2)}, u32[]{:S(2)}) async-start(bf16[16,24,1024]{2,1,0:T(8,128)(2,1)} %bitcast.12), calls=%async_computation | async-start | bytes 1572864 | tf_op jit(solution)/shard_map/all_to_all | solution.py:266
  38.9 8.7 %collective-permute-start.6 = (bf16[5,8,896]{2,1,0:T(8,128)(2,1)}, bf16[5,8,896]{2,1,0:T(8,128)(2,1)S(1)}, u32[]{:S(2)}, u32[]{:S(2)}) collective-permute-start(bf16[5,8,896]{2,1,0:T(8,128)(2,1)} %get-tuple-element.17), channel_id=1, source_target_pairs={{0,16},{16,0},{1,17},{17,1},{2,18},{18,2},{3,19},{19,3},{4,20},{20... | collective-permute-start | bytes 215048 | tf_op jit(solution)/shard_map/ppermute | solution.py:262
  48.5 1.7 copy-start.5
  50.3 7.1 %copy-start.1 = (bf16[256,2048]{1,0:T(8,128)(2,1)S(1)}, bf16[256,2048]{1,0:T(8,128)(2,1)}, u32[]{:S(2)}) copy-start(bf16[256,2048]{1,0:T(8,128)(2,1)} %q_ref.3) | copy-start | bytes 3145732
  50.3 63.6 %all-to-all-start.2 = ((bf16[16,2,5,8,896]{4,3,2,1,0:T(8,128)(2,1)}), bf16[16,2,5,8,896]{4,3,2,1,0:T(8,128)(2,1)S(1)}, u32[]{:S(2)}, u32[]{:S(2)}) async-start(bf16[16,2,5,8,896]{4,3,2,1,0:T(8,128)(2,1)} %broadcast_in_dim.10), calls=%async_computation.2 | async-start | bytes 4587520 | tf_op jit(solution)/shard_map/all_to_all | solution.py:266
  57.3 43.0 %collective-permute-start.1 = (bf16[256,2048]{1,0:T(8,128)(2,1)S(1)}, bf16[256,2048]{1,0:T(8,128)(2,1)S(1)}, u32[]{:S(2)}, u32[]{:S(2)}) collective-permute-start(bf16[256,2048]{1,0:T(8,128)(2,1)S(1)} %copy-done.1), channel_id=1, source_target_pairs={{0,16},{16,0},{1,17},{17,1},{2,18},{18,2},{3,19},{19,3},{4,20},{20... | collective-permute-start | bytes 3145736 | tf_op jit(solution)/shard_map/ppermute | solution.py:262
  62.1 39.3 %collective-permute-start.2 = (bf16[256,2048]{1,0:T(8,128)(2,1)}, bf16[256,2048]{1,0:T(8,128)(2,1)S(1)}, u32[]{:S(2)}, u32[]{:S(2)}) collective-permute-start(bf16[256,2048]{1,0:T(8,128)(2,1)} %g_ref.3), channel_id=1, source_target_pairs={{0,16},{16,0},{1,17},{17,1},{2,18},{18,2},{3,19},{19,3},{4,20},{20... | collective-permute-start | bytes 3145736 | tf_op jit(solution)/shard_map/ppermute | solution.py:262
  64.0 21.7 %collective-permute-start.3 = (bf16[2,128,896]{2,1,0:T(8,128)(2,1)}, bf16[2,128,896]{2,1,0:T(8,128)(2,1)S(1)}, u32[]{:S(2)}, u32[]{:S(2)}) collective-permute-start(bf16[2,128,896]{2,1,0:T(8,128)(2,1)} %param.8), channel_id=1, source_target_pairs={{18,0},{2,1},{20,2},{4,3},{22,4},{6,5},{24,6},{8,7},{26,8},{10,9},... | collective-permute-start | bytes 1376264 | tf_op jit(solution)/shard_map/ppermute | solution.py:285
  70.3 32.2 %collective-permute-start = (bf16[384,1024]{1,0:T(8,128)(2,1)}, bf16[384,1024]{1,0:T(8,128)(2,1)}, u32[]{:S(2)}, u32[]{:S(2)}) collective-permute-start(bf16[384,1024]{1,0:T(8,128)(2,1)} %bitcast.10), channel_id=1, source_target_pairs={{0,16},{16,0},{1,17},{17,1},{2,18},{18,2},{3,19},{19,3},{4,20},{20... | collective-permute-start | bytes 2359304 | tf_op jit(solution)/shard_map/ppermute | solution.py:262
  72.2 19.2 %collective-permute-start.4 = (bf16[2,128,896]{2,1,0:T(8,128)(2,1)}, bf16[2,128,896]{2,1,0:T(8,128)(2,1)S(1)}, u32[]{:S(2)}, u32[]{:S(2)}) collective-permute-start(bf16[2,128,896]{2,1,0:T(8,128)(2,1)} %param.8), channel_id=1, source_target_pairs={{30,0},{0,1},{16,2},{2,3},{18,4},{4,5},{20,6},{6,7},{22,8},{8,9},{... | collective-permute-start | bytes 1376264 | tf_op jit(solution)/shard_map/ppermute | solution.py:285
  85.7 15.6 %copy-start.7 = (bf16[2,128,896]{2,1,0:T(8,128)(2,1)}, bf16[2,128,896]{2,1,0:T(8,128)(2,1)S(1)}, u32[]{:S(2)}) copy-start(bf16[2,128,896]{2,1,0:T(8,128)(2,1)S(1)} %collective-permute-done.3.w0_ref) | copy-start | bytes 1376260
  85.7 14.6 %collective-permute-start.5 = (bf16[2,128,896]{2,1,0:T(8,128)(2,1)}, bf16[2,128,896]{2,1,0:T(8,128)(2,1)S(1)}, u32[]{:S(2)}, u32[]{:S(2)}) collective-permute-start(bf16[2,128,896]{2,1,0:T(8,128)(2,1)} %param.8), channel_id=1, source_target_pairs={{0,0},{20,1},{2,2},{22,3},{4,4},{24,5},{6,6},{26,7},{8,8},{28,9},{... | collective-permute-start | bytes 1376264 | tf_op jit(solution)/shard_map/ppermute | solution.py:285
  91.4 10.0 %copy-start.8 = (bf16[2,128,896]{2,1,0:T(8,128)(2,1)}, bf16[2,128,896]{2,1,0:T(8,128)(2,1)S(1)}, u32[]{:S(2)}) copy-start(bf16[2,128,896]{2,1,0:T(8,128)(2,1)S(1)} %collective-permute-done.4.w1_ref) | copy-start | bytes 1376260
  100.3 1.1 copy-start.9
  100.4 1.0 copy-start.2
  101.5 1.0 copy-start.3
  113.9 1.5 copy-start
  130.2 28.4 %all-to-all-start.3 = ((bf16[16,8,8,896]{3,2,1,0:T(8,128)(2,1)}), bf16[16,8,8,896]{3,2,1,0:T(8,128)(2,1)S(1)}, u32[]{:S(2)}, u32[]{:S(2)}) async-start(bf16[16,8,8,896]{3,2,1,0:T(8,128)(2,1)} %get-tuple-element.23), calls=%async_computation.3 | async-start | bytes 3670016 | tf_op jit(solution)/shard_map/all_to_all | solution.py:266
  137.1 30.4 %copy-start.4 = (bf16[256,2048]{1,0:T(8,128)(2,1)S(1)}, bf16[256,2048]{1,0:T(8,128)(2,1)}, u32[]{:S(2)}) copy-start(bf16[256,2048]{1,0:T(8,128)(2,1)} %get-tuple-element.21) | copy-start | bytes 3145732
  137.1 30.3 %collective-permute-start.7 = (bf16[256,2048]{1,0:T(8,128)(2,1)}, bf16[256,2048]{1,0:T(8,128)(2,1)}, u32[]{:S(2)}, u32[]{:S(2)}) collective-permute-start(bf16[256,2048]{1,0:T(8,128)(2,1)} %get-tuple-element.22), channel_id=1, source_target_pairs={{0,16},{16,0},{1,17},{17,1},{2,18},{18,2},{3,19},{19,3},{4,20},{20... | collective-permute-start | bytes 3145736 | tf_op jit(solution)/shard_map/ppermute | solution.py:262
  161.1 18.8 %all-to-all-start.4 = ((bf16[16,8,896]{2,1,0:T(8,128)(2,1)}), bf16[16,8,896]{2,1,0:T(8,128)(2,1)S(1)}, u32[]{:S(2)}, u32[]{:S(2)}) async-start(bf16[16,8,896]{2,1,0:T(8,128)(2,1)} %arrange.1), calls=%async_computation.4 | async-start | bytes 458752 | tf_op jit(solution)/shard_map/all_to_all | solution.py:266
  180.8 20.7 %all-to-all-start.5 = ((bf16[32,8,896]{2,1,0:T(8,128)(2,1)}), bf16[32,8,896]{2,1,0:T(8,128)(2,1)S(1)}, u32[]{:S(2)}, u32[]{:S(2)}) async-start(bf16[32,8,896]{2,1,0:T(8,128)(2,1)} %broadcast_in_dim.22), calls=%async_computation.5 | async-start | bytes 917504 | tf_op jit(solution)/shard_map/all_to_all | solution.py:266
